TPU v7x, 32 devices: a whole 2x2x4 slice. The times are simulated.
32 devices in a mesh: samp: 8 (over y, x, core), blk: 4 (over z).
Axes of the slice: x: 2, y: 2, z: 4, core: 2. Of those that a mesh axis runs over, the one named last changes fastest.
Arguments:
- genotypes: int32 [16384, 6144], P('samp', 'blk'), may hold values from 0 to 2
- phenotype: float32 [16384], P('samp'), may hold values from -15 to 15
- fold_ids: int32 [16384], P('samp'), may hold values from 0 to 4, as said below
Outputs:
- coeff_all: float32 [6144, 400], P('blk')
- fold_scores: float32 [2, 400], replicated
Inputs may be any that keep to these rules, and one draw needn't show every extreme that they name: `fold_ids`: every fold holds 3276 or 3277 people.
All inputs are finite; a program needn't handle non-finite values.
Results may differ from a plain program's by a relative error of at most 0.0003.
Values sent between devices are 32-bit elements; how exact they have to be, the bound alone decides.
A program may use at most 128 MiB of HBM per device.

v0:
```python
import math
import jax
import jax.numpy as jnp
from jax import lax
from jax.sharding import PartitionSpec as P

FOLDS = 5
LAMBDAS = 20
SWEEPS = 3
GRID = 400
step_size = 0.6
epsilon = 1e-05
lambda_base = 0.1
lambda_ratio = 1.2
shrink_unit = 0.2
highest = lax.Precision.HIGHEST


def grid_tables():
    column = jnp.arange(GRID)
    fold_of = column % FOLDS
    levels = column // FOLDS % LAMBDAS
    penalty = lambda_base * jnp.exp(levels.astype(jnp.float32) * math.log(lambda_ratio))
    shrink = shrink_unit * (column // (FOLDS * LAMBDAS) + 1).astype(jnp.float32)
    return (fold_of, penalty, shrink)


def soft_threshold(values, cutoff):
    return values - jnp.clip(values, -cutoff, cutoff)


def local(genotypes, phenotype, fold_ids):
    num_rows, block_width = genotypes.shape
    sample_count = num_rows * lax.axis_size("samp")
    snp_total = block_width * lax.axis_size("blk")
    dosage_bf = genotypes.astype(jnp.bfloat16)
    onehot = fold_ids[:, None] == jnp.arange(FOLDS)[None, :]
    pheno_split = jnp.where(onehot, phenotype[:, None], 0.0)
    local_sum = jnp.sum(genotypes, axis=0).astype(jnp.float32)
    local_sq = jnp.sum(genotypes * genotypes, axis=0).astype(jnp.float32)
    local_geno_pheno = jnp.dot(pheno_split.T, genotypes.astype(jnp.float32), precision=highest)
    local_pheno_sum = jnp.sum(pheno_split, axis=0)
    local_count = jnp.sum(onehot.astype(jnp.int32), axis=0).astype(jnp.float32)
    fold_of, penalty, shrink = grid_tables()
    column_fold = fold_of[None, :] == jnp.arange(FOLDS)[:, None]
    gram_local = jnp.dot(dosage_bf.T, dosage_bf, preferred_element_type=jnp.float32)
    gram_sum, geno_sum, geno_sq, geno_pheno, fold_pheno_sum, fold_count = lax.psum(
        (gram_local, local_sum, local_sq, local_geno_pheno, local_pheno_sum, local_count), "samp"
    )
    snp_mean = geno_sum / sample_count
    scales = jnp.sqrt(geno_sq / sample_count - snp_mean * snp_mean + epsilon)
    train_geno = jnp.sum(geno_pheno, axis=0)[None, :] - geno_pheno
    train_pheno = jnp.sum(fold_pheno_sum) - fold_pheno_sum
    zscore = (train_geno - train_pheno[:, None] * snp_mean[None, :]) / (
        scales[None, :] * jnp.sqrt(sample_count - fold_count)[:, None]
    )
    snp_mean, scales, zscore = (snp_mean, scales, zscore)
    ld_block = (gram_sum / sample_count - snp_mean[:, None] * snp_mean[None, :]) / (
        scales[:, None] * scales[None, :]
    )
    col_share = GRID // lax.axis_size("samp")
    first_col = lax.axis_index("samp") * col_share
    target = lax.dynamic_slice_in_dim(
        jnp.sum(jnp.where(column_fold[None, :, :], zscore.T[:, :, None], 0.0), axis=1),
        first_col,
        col_share,
        1,
    )
    penalty_mine = lax.dynamic_slice_in_dim(penalty, first_col, col_share, 0)
    shrink_mine = lax.dynamic_slice_in_dim(shrink, first_col, col_share, 0)
    coeffs = soft_threshold(step_size * target, step_size * penalty_mine)
    for sweep_idx in range(SWEEPS - 1):
        gradient = (
            (1.0 - shrink_mine) * jnp.dot(ld_block, coeffs, precision=highest)
            + shrink_mine * coeffs
            - target
        )
        coeffs = soft_threshold(coeffs - step_size * gradient, step_size * penalty_mine)
    coeff_all = lax.all_gather(coeffs, "samp", axis=1, tiled=True)
    weighted = (coeff_all / scales[:, None]).astype(jnp.bfloat16)
    offset = jnp.dot(snp_mean[None, :], weighted.astype(jnp.float32), precision=highest)
    partial_value = jnp.dot(dosage_bf, weighted, preferred_element_type=jnp.float32) - offset
    root_snps = math.sqrt(snp_total)
    col_part = GRID // lax.axis_size("blk")
    part_first = lax.axis_index("blk") * col_part
    predicted = lax.psum_scatter(partial_value, "blk", scatter_dimension=1, tiled=True) / root_snps
    fold_slice = lax.dynamic_slice_in_dim(fold_of, part_first, col_part, 0)
    chosen = fold_ids[:, None] == fold_slice[None, :]
    numerator = jnp.sum(jnp.where(chosen, predicted * phenotype[:, None], 0.0), axis=0)
    denominator = jnp.sum(jnp.where(chosen, predicted * predicted, 0.0), axis=0)
    numerator, denominator = lax.psum((numerator, denominator), "samp")
    slice_fold = fold_slice[None, :] == jnp.arange(FOLDS)[:, None]
    counts = jnp.sum(jnp.where(slice_fold, fold_count[:, None], 0.0), axis=0)
    piece_scores = jnp.stack([numerator / counts, denominator / counts])
    fold_scores = lax.all_gather(piece_scores, "blk", axis=1, tiled=True)
    return (coeff_all, fold_scores)


def solution(mesh):
    return jax.shard_map(
        local,
        mesh=mesh,
        in_specs=(P("samp", "blk"), P("samp"), P("samp")),
        out_specs=(P("blk", None), P()),
        check_vma=False,
    )
```

profile of v0, /device:TPU:0, one launch (start us, length us, event | category | flops | bytes accessed | tf_op | source)
XLA Modules:
  0.0 336.0 jit_solution(6285634921455484251)
XLA Ops:
  7.2 0.0 all-reduce.6.cloned.1.call-start
  7.2 19.0 %fusion.5 = f32[1536,1536]{1,0:T(8,128)} fusion(s32[2048,1536]{1,0:T(8,128)} %param.3), kind=kOutput, calls=%fused_computation.8 | convolution fusion | flops 9666822144 | bytes 22020096 | tf_op jit(solution)/shard_map/dot_general | solution.py:46
  26.2 0.0 copy-start.2
  26.2 0.0 copy-start.3
  26.2 0.0 all-reduce.6.cloned.1.call-update
  26.2 0.2 all-gather.4.cloned.1.call-start
  26.5 0.0 copy-start
  26.5 6.1 %fusion.53 = (s32[1536]{0:T(1024)S(1)}, s32[1536]{0:T(1024)S(1)}) fusion(s32[2048,1536]{1,0:T(8,128)} %param.3), kind=kLoop, calls=%fused_computation.86 | loop fusion | flops 9434112 | bytes 12595200 | tf_op jit(solution)/shard_map/reduce_sum | solution.py:39
  32.6 0.0 copy-done.2
  32.6 0.1 convert_reduce_fusion
  32.7 0.0 copy-done.3
  32.7 0.1 select_reduce_fusion.1
  32.8 1.9 copy-done
  34.7 6.2 %fusion.1 = f32[5,1536]{1,0:T(8,128)S(1)} fusion(s32[2048,1536]{1,0:T(8,128)S(1)} %copy-done, f32[2048]{0:T(1024)S(1)} %copy-done.3, s32[2048]{0:T(1024)S(1)} %copy-done.2), kind=kOutput, calls=%fused_computation.1 | convolution fusion | flops 191909888 | bytes 12630016 | tf_op jit(solution)/shard_map/dot_general | solution.py:41
  41.0 30.4 %all-reduce.3 = (f32[1536]{0:T(1024)S(1)}, f32[1536]{0:T(1024)S(1)}, f32[5,1536]{1,0:T(8,128)S(1)}, f32[5]{0:T(128)S(1)}, f32[5]{0:T(128)S(1)}) all-reduce(f32[1536]{0:T(1024)S(1)} %convert_element_type.30, f32[1536]{0:T(1024)S(1)} %convert_element_type.29, f32[5,1536]{1,0:T(8,128)S(1)} %fusion.1, ...), channel_id=1, replica_groups=mesh['samp'=8,'blk'=4] {'samp'}, use_global_device_ids=true, to_apply=%region_8.9 | all-reduce | flops 10762 | bytes 86096 | tf_op jit(solution)/shard_map/psum | solution.py:47
  71.3 0.6 reduce_sum.92
  72.0 0.1 broadcast_subtract_fusion
  72.1 0.7 subtract_sqrt_fusion
  72.8 0.1 divide_bitcast_fusion
  72.9 0.9 select_reduce_fusion
  73.8 94.8 %all-reduce.6.cloned.1.call-done = f32[1536,1536]{1,0:T(8,128)} async-done(((f32[1536,1536]{1,0:T(8,128)}), f32[1536,1536]{1,0:T(8,128)}) %all-reduce.6.cloned.1.call-update) | async-done | bytes 9437200 | tf_op jit(solution)/shard_map/psum | solution.py:47
  168.6 5.4 %multiply_divide_fusion = f32[1536,1536]{1,0:T(8,128)S(1)} fusion(f32[1536,1536]{1,0:T(8,128)} %all-reduce.6.cloned.1.call-done, f32[1536]{0:T(1024)S(1)} %get-tuple-element.18, f32[1536]{0:T(1024)S(1)} %get-tuple-element.17), kind=kLoop, calls=%fused_computation.4 | loop fusion | flops 11796480 | bytes 18886656 | tf_op jit(solution)/shard_map/div | solution.py:58
  174.0 0.0 copy-start.4
  174.0 9.2 %fusion.14 = f32[1536,50]{0,1:T(8,128)S(1)} fusion(f32[1536,1536]{1,0:T(8,128)S(1)} %multiply_divide_fusion, f32[1536,400]{0,1:T(8,128)S(1)} %select_reduce_fusion, s32[]{:T(128)S(6)} %select_n.55, f32[50]{0:T(128)S(1)} %get-tuple-element.16, f32[50]{0:T(128)S(1)} %get-tuple-element.15, f32[50]{0:T(128)S(1)} %get-tuple-element.23, f32[50]{0:T(128)S(1)} %get-tuple-element.24), kind=kOutput, calls=%fused_computation.18 | convolution fusion | flops 1416652800 | bytes 10436608 | tf_op jit(solution)/shard_map/dot_general | solution.py:74
  183.3 10.2 %subtract_bitcast_fusion.1 = f32[1,50,1536]{2,1,0:T(8,128)} fusion(f32[1536,1536]{1,0:T(8,128)S(1)} %multiply_divide_fusion, f32[1536,50]{0,1:T(8,128)S(1)} %fusion.14, f32[1536,400]{0,1:T(8,128)S(1)} %select_reduce_fusion, s32[]{:T(128)S(6)} %select_n.55, f32[50]{0:T(128)S(1)} %get-tuple-element.16, f32[50]{0:T(128)S(1)} %get-tuple-element.15, ...), kind=kOutput, calls=%fused_computation.25 | convolution fusion | flops 1416729600 | bytes 10779652 | tf_op jit(solution)/shard_map/dot_general | solution.py:74
  193.5 0.0 all-gather.4.cloned.1.call-update
  193.6 0.1 dynamic_slice.15
  193.6 0.0 copy-done.4
  193.6 0.6 dynamic-slice.4
  194.9 29.4 %all-gather.4.cloned.1.call-done = f32[8,50,1536]{2,1,0:T(8,128)} async-done(((f32[1,50,1536]{2,1,0:T(8,128)}), f32[8,50,1536]{2,1,0:T(8,128)}) %all-gather.4.cloned.1.call-update) | async-done | bytes 2457616 | tf_op jit(solution)/shard_map/all_gather | solution.py:79
  224.3 1.9 reshape.54
  226.2 0.0 copy-start.1
  226.2 0.2 divide_convert_fusion
  226.5 1.0 fusion.55
  227.5 9.0 %subtract_bitcast_fusion = f32[2048,400]{0,1:T(8,128)} fusion(bf16[1536,400]{0,1:T(8,128)(2,1)S(1)} %divide_convert_fusion, s32[2048,1536]{1,0:T(8,128)} %param.3, f32[400]{0:T(512)S(1)} %bitcast.32), kind=kOutput, calls=%fused_computation.5 | convolution fusion | flops 2520547328 | bytes 17090112 | tf_op jit(solution)/shard_map/dot_general | solution.py:82
  236.5 0.0 copy-done.1
  236.5 65.2 %fusion = f32[2048,104]{0,1:T(8,128)S(1)} fusion(f32[2048,400]{0,1:T(8,128)} %subtract_bitcast_fusion), kind=kCustom, calls=%all-reduce-scatter | all-reduce-scatter fusion | flops 851969 | bytes 4129280
  301.8 1.3 collective-permute-start
  303.1 0.1 select_reduce_fusion.2
  303.2 2.4 collective-permute-done
  305.6 0.5 concatenate
  306.0 0.4 fusion.17
  306.4 11.8 %all-reduce.2 = (f32[100]{0:T(128)S(1)}, f32[100]{0:T(128)S(1)}) all-reduce(f32[100]{0:T(128)S(1)} %get-tuple-element.5, f32[100]{0:T(128)S(1)} %get-tuple-element.4), channel_id=1, replica_groups=mesh['samp'=8,'blk'=4] {'samp'}, use_global_device_ids=true, to_apply=%region_18.19 | all-reduce | flops 200 | bytes 1600 | tf_op jit(solution)/shard_map/psum | solution.py:91
  318.3 10.2 %all-gather.1 = f32[4,100,2]{1,2,0:T(2,128)S(1)} all-gather(f32[1,100,2]{1,2,0:T(2,128)S(1)} %maximum_bitcast_fusion), channel_id=1, replica_groups=mesh['samp'=8,'blk'=4] {'blk'}, dimensions={0}, use_global_device_ids=true | all-gather | bytes 4000 | tf_op jit(solution)/shard_map/all_gather | solution.py:95
  328.5 0.7 reshape.56
  (15 shorter events, 0.1 us)
Async XLA Ops:
  7.2 161.4 %all-reduce.6.cloned.1.call-start = ((), (), s32[]{:S(2)}) async-start(), calls=%async_computation | async-start | bytes 18874368 | tf_op jit(solution)/shard_map/psum | solution.py:47
  26.2 6.4 %copy-start.2 = (s32[2048]{0:T(1024)S(1)}, s32[2048]{0:T(1024)}, u32[]{:S(2)}) copy-start(s32[2048]{0:T(1024)} %param.5) | copy-start | bytes 24580
  26.2 6.5 %copy-start.3 = (f32[2048]{0:T(1024)S(1)}, f32[2048]{0:T(1024)}, u32[]{:S(2)}) copy-start(f32[2048]{0:T(1024)} %param.4) | copy-start | bytes 24580
  26.2 198.1 %all-gather.4.cloned.1.call-start = ((), (), s32[]{:S(2)}) async-start(), calls=%async_computation.1 | async-start | bytes 3096576 | tf_op jit(solution)/shard_map/all_gather | solution.py:79
  26.5 8.3 %copy-start = (s32[2048,1536]{1,0:T(8,128)S(1)}, s32[2048,1536]{1,0:T(8,128)}, u32[]{:S(2)}) copy-start(s32[2048,1536]{1,0:T(8,128)} %param.3) | copy-start | bytes 37748740
  174.0 19.6 %copy-start.4 = (u32[32]{0:T(128)S(1)}, u32[32]{0:T(128)}, u32[]{:S(2)}) copy-start(u32[32]{0:T(128)} %constant.77) | copy-start | bytes 388
  226.2 10.3 %copy-start.1 = (f32[400,1536]{1,0:T(8,128)}, f32[400,1536]{1,0:T(8,128)S(1)}, u32[]{:S(2)}) copy-start(f32[400,1536]{1,0:T(8,128)S(1)} %reshape.54) | copy-start | bytes 7372804
  301.8 3.8 %collective-permute-start = (f32[2048,12]{0,1:T(8,128)S(1)}, f32[2048,12]{0,1:T(8,128)S(1)}, u32[]{:S(2)}, u32[]{:S(2)}) collective-permute-start(f32[2048,12]{0,1:T(8,128)S(1)} %slice), channel_id=1, source_target_pairs={{0,1},{1,2},{2,3},{4,5},{5,6},{6,7},{8,9},{9,10},{10,11},{12,13},{... | collective-permute-start | bytes 294920
Sparse Core Ops, SparseCore 0:
  26.3 142.1 all-reduce.5
  193.6 30.5 all-gather.3
where the time goes:
time: 336 us
  waiting for transfers between devices  127 us (38%)
  blocking collectives  118 us (35%)
  matrix products  54.8 us (16%)
  other arithmetic  15 us (4%)
  between operations  14.9 us (4%)
  local copies, waits for them, and re-layouts  5.64 us (2%)
    psum x1, waiting for transfers between devices, local(): lax.psum((gram_local, local_sum, local_sq, local_geno_pheno, local_pheno_...  94.8 us
    unnamed x1, blocking collectives  65.2 us
    psum x1, blocking collectives, local(): lax.psum((gram_local, local_sum, local_sq, local_geno_pheno, local_pheno_...  30.4 us
    all_gather x1, waiting for transfers between devices, local(): coeff_all = lax.all_gather(coeffs, 'samp', axis=1, tiled=True)  29.4 us
    dot_general x2, matrix products, local(): jnp.dot(ld_block, coeffs, precision=highest)  19.5 us
    dot_general x1, matrix products, local(): jnp.dot(dosage_bf.T, dosage_bf, preferred_element_type=jnp.float32)  19 us
    psum x1, blocking collectives, local(): numerator, denominator = lax.psum((numerator, denominator), 'samp')  11.8 us
    all_gather x1, blocking collectives, local(): fold_scores = lax.all_gather(piece_scores, 'blk', axis=1, tiled=True)  10.2 us
  transfers between devices with their start and end apart: 3, of which 3 were waited for; matrix products, arithmetic and copies ran while one was open for 5% of the time, Pallas kernels for 0%

commit v1 on v0

--- a/solution.py
+++ b/solution.py
@@ -76,7 +76,16 @@
             - target
         )
         coeffs = soft_threshold(coeffs - step_size * gradient, step_size * penalty_mine)
-    coeff_all = lax.all_gather(coeffs, "samp", axis=1, tiled=True)
+    ways = lax.axis_size("samp")
+    up = [(d, (d + 1) % ways) for d in range(ways)]
+    down = [(d, (d - 1) % ways) for d in range(ways)]
+    earlier, later = ([coeffs], [coeffs])
+    for _ in range(ways // 2):
+        earlier.append(lax.ppermute(earlier[-1], "samp", up))
+    for _ in range((ways - 1) // 2):
+        later.append(lax.ppermute(later[-1], "samp", down))
+    line = jnp.concatenate([*earlier[::-1], *later[1:]], axis=1)
+    coeff_all = jnp.roll(line, (lax.axis_index("samp") - ways // 2) * coeffs.shape[1], axis=1)
     weighted = (coeff_all / scales[:, None]).astype(jnp.bfloat16)
     offset = jnp.dot(snp_mean[None, :], weighted.astype(jnp.float32), precision=highest)
     partial_value = jnp.dot(dosage_bf, weighted, preferred_element_type=jnp.float32) - offset

time: 336 us -> 369 us (1.098); the launches traced: 336 us -> 364 us
  local copies, waits for them, and re-layouts: 5.64 us -> 25.8 us
  starting transfers between devices: 1.56 us -> 11 us
  blocking collectives: 118 us -> 111 us
    ppermute x0 -> x7, waiting for transfers between devices: none -> 30.5 us  [the longest x4 30.5 us: local(): earlier.append(lax.ppermute(earlier[-1], 'samp', up))]
    all_gather x1 -> x0, waiting for transfers between devices: 29.4 us -> none  [local(): coeff_all = lax.all_gather(coeffs, 'samp', axis=1, tiled=True)]
    concatenate x0 -> x1, local copies, waits for them, and re-layouts: none -> 22.2 us  [local(): jnp.roll(line, (lax.axis_index('samp') - ways // 2) * coeffs.shape[1], ax...]
    ppermute x0 -> x7, starting transfers between devices: none -> 7.98 us  [the longest x3 7.92 us: local(): later.append(lax.ppermute(later[-1], 'samp', down))]
    unnamed x1, blocking collectives: 65.2 us -> 58.6 us
  transfers between devices with their start and end apart: 3 -> 9, of which waited for: 3 -> 6; matrix products, arithmetic and copies ran while one was open for 5% -> 4% of each run, Pallas kernels for 0% -> 0%
where the time goes in v1:
time: 369 us; the launch traced here: 364 us
  waiting for transfers between devices  128 us (35%)
  blocking collectives  111 us (30%)
  matrix products  54.5 us (15%)
  local copies, waits for them, and re-layouts  25.8 us (7%)
  other arithmetic  18.3 us (5%)
  between operations  15.2 us (4%)
  starting transfers between devices  11 us (3%)
    psum x1, waiting for transfers between devices, local(): lax.psum((gram_local, local_sum, local_sq, local_geno_pheno, local_pheno_...  95.2 us
    unnamed x1, blocking collectives  58.6 us
    ppermute x4, waiting for transfers between devices, local(): earlier.append(lax.ppermute(earlier[-1], 'samp', up))  30.5 us
    psum x1, blocking collectives, local(): lax.psum((gram_local, local_sum, local_sq, local_geno_pheno, local_pheno_...  30.3 us
    concatenate x1, local copies, waits for them, and re-layouts, local(): jnp.roll(line, (lax.axis_index('samp') - ways // 2) * coeffs.shape[1], ax...  22.2 us
    dot_general x1, matrix products, local(): jnp.dot(dosage_bf.T, dosage_bf, preferred_element_type=jnp.float32)  19.4 us
    dot_general x2, matrix products, local(): jnp.dot(ld_block, coeffs, precision=highest)  18.7 us
    psum x1, blocking collectives, local(): numerator, denominator = lax.psum((numerator, denominator), 'samp')  11.8 us
  transfers between devices with their start and end apart: 9, of which 6 were waited for; matrix products, arithmetic and copies ran while one was open for 4% of the time, Pallas kernels for 0%

profile of v1, /device:TPU:0, one launch (start us, length us, event | category | flops | bytes accessed | tf_op | source)
XLA Modules:
  0.0 363.6 jit_solution(5165685055051787495)
XLA Ops:
  7.2 0.0 all-reduce.6.cloned.1.call-start
  7.2 19.4 %fusion.5 = f32[1536,1536]{1,0:T(8,128)} fusion(s32[2048,1536]{1,0:T(8,128)} %param.3), kind=kOutput, calls=%fused_computation.8 | convolution fusion | flops 9666822144 | bytes 22020096 | tf_op jit(solution)/shard_map/dot_general | solution.py:46
  26.6 0.0 copy-start.1
  26.7 0.0 copy-start.2
  26.7 0.0 all-reduce.6.cloned.1.call-update
  26.7 0.0 copy-start
  26.7 6.1 %fusion.53 = (s32[1536]{0:T(1024)S(1)}, s32[1536]{0:T(1024)S(1)}) fusion(s32[2048,1536]{1,0:T(8,128)} %param.3), kind=kLoop, calls=%fused_computation.87 | loop fusion | flops 9434112 | bytes 12595200 | tf_op jit(solution)/shard_map/reduce_sum | solution.py:39
  32.8 0.1 convert_reduce_fusion
  33.0 0.1 select_reduce_fusion.1
  33.1 1.8 copy-done
  34.9 6.2 %fusion.1 = f32[5,1536]{1,0:T(8,128)S(1)} fusion(s32[2048,1536]{1,0:T(8,128)S(1)} %copy-done, f32[2048]{0:T(1024)S(1)} %copy-done.2, s32[2048]{0:T(1024)S(1)} %copy-done.1), kind=kOutput, calls=%fused_computation.1 | convolution fusion | flops 191909888 | bytes 12630016 | tf_op jit(solution)/shard_map/dot_general | solution.py:41
  41.1 30.3 %all-reduce.3 = (f32[1536]{0:T(1024)S(1)}, f32[1536]{0:T(1024)S(1)}, f32[5,1536]{1,0:T(8,128)S(1)}, f32[5]{0:T(128)S(1)}, f32[5]{0:T(128)S(1)}) all-reduce(f32[1536]{0:T(1024)S(1)} %convert_element_type.30, f32[1536]{0:T(1024)S(1)} %convert_element_type.29, f32[5,1536]{1,0:T(8,128)S(1)} %fusion.1, ...), channel_id=1, replica_groups=mesh['samp'=8,'blk'=4] {'samp'}, use_global_device_ids=true, to_apply=%region_8.9 | all-reduce | flops 10762 | bytes 86096 | tf_op jit(solution)/shard_map/psum | solution.py:47
  71.4 0.6 reduce_sum.92
  72.1 0.1 broadcast_subtract_fusion
  72.2 0.7 subtract_sqrt_fusion
  72.9 0.1 divide_bitcast_fusion
  73.0 0.9 select_reduce_fusion
  73.9 95.2 %all-reduce.6.cloned.1.call-done = f32[1536,1536]{1,0:T(8,128)} async-done(((f32[1536,1536]{1,0:T(8,128)}), f32[1536,1536]{1,0:T(8,128)}) %all-reduce.6.cloned.1.call-update) | async-done | bytes 9437200 | tf_op jit(solution)/shard_map/psum | solution.py:47
  169.1 5.4 %multiply_divide_fusion = f32[1536,1536]{1,0:T(8,128)S(1)} fusion(f32[1536,1536]{1,0:T(8,128)} %all-reduce.6.cloned.1.call-done, f32[1536]{0:T(1024)S(1)} %get-tuple-element.20, f32[1536]{0:T(1024)S(1)} %get-tuple-element.19), kind=kLoop, calls=%fused_computation.4 | loop fusion | flops 11796480 | bytes 18886656 | tf_op jit(solution)/shard_map/div | solution.py:58
  174.5 0.0 copy-start.3
  174.5 9.2 %fusion.14 = f32[1536,50]{0,1:T(8,128)S(1)} fusion(f32[1536,1536]{1,0:T(8,128)S(1)} %multiply_divide_fusion, f32[1536,400]{0,1:T(8,128)S(1)} %select_reduce_fusion, s32[]{:T(128)S(6)} %select_n.67, f32[50]{0:T(128)S(1)} %get-tuple-element.18, f32[50]{0:T(128)S(1)} %get-tuple-element.17, f32[50]{0:T(128)S(1)} %get-tuple-element.25, f32[50]{0:T(128)S(1)} %get-tuple-element.26), kind=kOutput, calls=%fused_computation.18 | convolution fusion | flops 1416652800 | bytes 10436608 | tf_op jit(solution)/shard_map/dot_general | solution.py:74
  183.7 9.5 %minimum_subtract_fusion = f32[1536,50]{0,1:T(8,128)S(1)} fusion(f32[1536,1536]{1,0:T(8,128)S(1)} %multiply_divide_fusion, f32[1536,50]{0,1:T(8,128)S(1)} %fusion.14, f32[1536,400]{0,1:T(8,128)S(1)} %select_reduce_fusion, s32[]{:T(128)S(6)} %select_n.67, f32[50]{0:T(128)S(1)} %get-tuple-element.18, f32[50]{0:T(128)S(1)} %get-tuple-element.17, ...), kind=kOutput, calls=%fused_computation.25 | convolution fusion | flops 1416729600 | bytes 10779652 | tf_op jit(solution)/shard_map/dot_general | solution.py:74
  193.3 0.1 collective-permute-start
  193.3 2.6 collective-permute-start.4
  196.0 7.7 %collective-permute-done = f32[1536,50]{0,1:T(8,128)S(1)} collective-permute-done((f32[1536,50]{0,1:T(8,128)S(1)}, f32[1536,50]{0,1:T(8,128)S(1)}, u32[]{:S(2)}, u32[]{:S(2)}) %collective-permute-start) | collective-permute-done | bytes 307232 | tf_op jit(solution)/shard_map/ppermute | solution.py:84
  203.6 0.0 collective-permute-start.1
  203.6 2.6 collective-permute-start.5
  206.3 8.5 %collective-permute-done.1 = f32[1536,50]{0,1:T(8,128)S(1)} collective-permute-done((f32[1536,50]{0,1:T(8,128)S(1)}, f32[1536,50]{0,1:T(8,128)S(1)}, u32[]{:S(2)}, u32[]{:S(2)}) %collective-permute-start.1) | collective-permute-done | bytes 307232 | tf_op jit(solution)/shard_map/ppermute | solution.py:84
  214.8 0.0 collective-permute-start.2
  214.8 2.6 collective-permute-start.6
  217.4 8.1 %collective-permute-done.2 = f32[1536,50]{0,1:T(8,128)S(1)} collective-permute-done((f32[1536,50]{0,1:T(8,128)S(1)}, f32[1536,50]{0,1:T(8,128)S(1)}, u32[]{:S(2)}, u32[]{:S(2)}) %collective-permute-start.2) | collective-permute-done | bytes 307232 | tf_op jit(solution)/shard_map/ppermute | solution.py:84
  225.6 0.0 collective-permute-start.3
  225.6 0.1 dynamic_slice.20
  225.7 0.6 dynamic-slice.4
  226.9 6.2 %collective-permute-done.3 = f32[1536,50]{0,1:T(8,128)S(1)} collective-permute-done((f32[1536,50]{0,1:T(8,128)S(1)}, f32[1536,50]{0,1:T(8,128)S(1)}, u32[]{:S(2)}, u32[]{:S(2)}) %collective-permute-start.3) | collective-permute-done | bytes 307232 | tf_op jit(solution)/shard_map/ppermute | solution.py:84
  233.1 22.2 %concatenate.6 = f32[1536,800]{0,1:T(8,128)} concatenate(f32[1536,50]{0,1:T(8,128)S(1)} %collective-permute-done.3, f32[1536,50]{0,1:T(8,128)S(1)} %collective-permute-done.2, f32[1536,50]{0,1:T(8,128)S(1)} %collective-permute-done.1, f32[1536,50]{0,1:T(8,128)S(1)} %collective-permute-done, f32[1536,50]{0,1:T(8,128)S(1)} %minimum_subtract_fusion, ...), dimensions={1} | concatenate | bytes 9830400 | tf_op jit(solution)/shard_map/jit(_roll_dynamic)/concatenate | solution.py:88
  255.3 3.6 divide_convert_fusion
  258.9 1.0 fusion.55
  260.0 9.0 %subtract_bitcast_fusion = f32[2048,400]{0,1:T(8,128)} fusion(bf16[1536,400]{0,1:T(8,128)(2,1)S(1)} %get-tuple-element.13, s32[2048,1536]{1,0:T(8,128)} %param.3, f32[400]{0:T(512)S(1)} %bitcast.25), kind=kOutput, calls=%fused_computation.5 | convolution fusion | flops 2520547328 | bytes 17090112 | tf_op jit(solution)/shard_map/dot_general | solution.py:91
  269.0 58.6 %fusion = f32[2048,104]{0,1:T(8,128)S(1)} fusion(f32[2048,400]{0,1:T(8,128)} %subtract_bitcast_fusion), kind=kCustom, calls=%all-reduce-scatter | all-reduce-scatter fusion | flops 851969 | bytes 4129280
  327.7 2.9 collective-permute-start.7
  330.6 0.1 select_reduce_fusion.2
  330.7 2.4 collective-permute-done.7
  333.1 0.5 concatenate.7
  333.6 0.4 fusion.17
  334.0 11.8 %all-reduce.2 = (f32[100]{0:T(128)S(1)}, f32[100]{0:T(128)S(1)}) all-reduce(f32[100]{0:T(128)S(1)} %get-tuple-element.5, f32[100]{0:T(128)S(1)} %get-tuple-element.4), channel_id=1, replica_groups=mesh['samp'=8,'blk'=4] {'samp'}, use_global_device_ids=true, to_apply=%region_18.19 | all-reduce | flops 200 | bytes 1600 | tf_op jit(solution)/shard_map/psum | solution.py:100
  345.8 10.0 %all-gather = f32[4,100,2]{1,2,0:T(2,128)S(1)} all-gather(f32[1,100,2]{1,2,0:T(2,128)S(1)} %maximum_bitcast_fusion), channel_id=1, replica_groups=mesh['samp'=8,'blk'=4] {'blk'}, dimensions={0}, use_global_device_ids=true | all-gather | bytes 4000 | tf_op jit(solution)/shard_map/all_gather | solution.py:104
  355.8 0.7 reshape.54
  (21 shorter events, 0.2 us)
Async XLA Ops:
  7.2 161.9 %all-reduce.6.cloned.1.call-start = ((), (), s32[]{:S(2)}) async-start(), calls=%async_computation | async-start | bytes 18874368 | tf_op jit(solution)/shard_map/psum | solution.py:47
  26.6 6.2 %copy-start.1 = (s32[2048]{0:T(1024)S(1)}, s32[2048]{0:T(1024)}, u32[]{:S(2)}) copy-start(s32[2048]{0:T(1024)} %param.5) | copy-start | bytes 24580
  26.7 6.3 %copy-start.2 = (f32[2048]{0:T(1024)S(1)}, f32[2048]{0:T(1024)}, u32[]{:S(2)}) copy-start(f32[2048]{0:T(1024)} %param.4) | copy-start | bytes 24580
  26.7 8.2 %copy-start = (s32[2048,1536]{1,0:T(8,128)S(1)}, s32[2048,1536]{1,0:T(8,128)}, u32[]{:S(2)}) copy-start(s32[2048,1536]{1,0:T(8,128)} %param.3) | copy-start | bytes 37748740
  174.5 51.2 %copy-start.3 = (u32[32]{0:T(128)S(1)}, u32[32]{0:T(128)}, u32[]{:S(2)}) copy-start(u32[32]{0:T(128)} %constant.97) | copy-start | bytes 388
  193.3 10.4 %collective-permute-start = (f32[1536,50]{0,1:T(8,128)S(1)}, f32[1536,50]{0,1:T(8,128)S(1)}, u32[]{:S(2)}, u32[]{:S(2)}) collective-permute-start(f32[1536,50]{0,1:T(8,128)S(1)} %minimum_subtract_fusion), channel_id=1, source_target_pairs={{0,4},{4,8},{8,12},{12,16},{16,20},{20,24},{24,28},{28,0},{1,5},{5... | collective-permute-start | bytes 921608 | tf_op jit(solution)/shard_map/ppermute | solution.py:84
  193.3 10.3 %collective-permute-start.4 = (f32[1536,50]{0,1:T(8,128)S(1)}, f32[1536,50]{0,1:T(8,128)S(1)}, u32[]{:S(2)}, u32[]{:S(2)}) collective-permute-start(f32[1536,50]{0,1:T(8,128)S(1)} %minimum_subtract_fusion), channel_id=1, source_target_pairs={{0,28},{4,0},{8,4},{12,8},{16,12},{20,16},{24,20},{28,24},{1,29},{... | collective-permute-start | bytes 921608 | tf_op jit(solution)/shard_map/ppermute | solution.py:86
  203.6 11.1 %collective-permute-start.1 = (f32[1536,50]{0,1:T(8,128)S(1)}, f32[1536,50]{0,1:T(8,128)S(1)}, u32[]{:S(2)}, u32[]{:S(2)}) collective-permute-start(f32[1536,50]{0,1:T(8,128)S(1)} %collective-permute-done), channel_id=1, source_target_pairs={{0,4},{4,8},{8,12},{12,16},{16,20},{20,24},{24,28},{28,0},{1,5},{5... | collective-permute-start | bytes 921608 | tf_op jit(solution)/shard_map/ppermute | solution.py:84
  203.6 11.1 %collective-permute-start.5 = (f32[1536,50]{0,1:T(8,128)S(1)}, f32[1536,50]{0,1:T(8,128)S(1)}, u32[]{:S(2)}, u32[]{:S(2)}) collective-permute-start(f32[1536,50]{0,1:T(8,128)S(1)} %collective-permute-done.4), channel_id=1, source_target_pairs={{0,28},{4,0},{8,4},{12,8},{16,12},{20,16},{24,20},{28,24},{1,29},{... | collective-permute-start | bytes 921608 | tf_op jit(solution)/shard_map/ppermute | solution.py:86
  214.8 10.8 %collective-permute-start.2 = (f32[1536,50]{0,1:T(8,128)S(1)}, f32[1536,50]{0,1:T(8,128)S(1)}, u32[]{:S(2)}, u32[]{:S(2)}) collective-permute-start(f32[1536,50]{0,1:T(8,128)S(1)} %collective-permute-done.1), channel_id=1, source_target_pairs={{0,4},{4,8},{8,12},{12,16},{16,20},{20,24},{24,28},{28,0},{1,5},{5... | collective-permute-start | bytes 921608 | tf_op jit(solution)/shard_map/ppermute | solution.py:84
  214.8 12.1 %collective-permute-start.6 = (f32[1536,50]{0,1:T(8,128)S(1)}, f32[1536,50]{0,1:T(8,128)S(1)}, u32[]{:S(2)}, u32[]{:S(2)}) collective-permute-start(f32[1536,50]{0,1:T(8,128)S(1)} %collective-permute-done.5), channel_id=1, source_target_pairs={{0,28},{4,0},{8,4},{12,8},{16,12},{20,16},{24,20},{28,24},{1,29},{... | collective-permute-start | bytes 921608 | tf_op jit(solution)/shard_map/ppermute | solution.py:86
  225.6 7.6 %collective-permute-start.3 = (f32[1536,50]{0,1:T(8,128)S(1)}, f32[1536,50]{0,1:T(8,128)S(1)}, u32[]{:S(2)}, u32[]{:S(2)}) collective-permute-start(f32[1536,50]{0,1:T(8,128)S(1)} %collective-permute-done.2), channel_id=1, source_target_pairs={{0,4},{4,8},{8,12},{12,16},{16,20},{20,24},{24,28},{28,0},{1,5},{5... | collective-permute-start | bytes 921608 | tf_op jit(solution)/shard_map/ppermute | solution.py:84
  327.7 5.4 %collective-permute-start.7 = (f32[2048,12]{0,1:T(8,128)S(1)}, f32[2048,12]{0,1:T(8,128)S(1)}, u32[]{:S(2)}, u32[]{:S(2)}) collective-permute-start(f32[2048,12]{0,1:T(8,128)S(1)} %slice), channel_id=1, source_target_pairs={{0,1},{1,2},{2,3},{4,5},{5,6},{6,7},{8,9},{9,10},{10,11},{12,13},{... | collective-permute-start | bytes 294920
Sparse Core Ops, SparseCore 0:
  26.8 142.2 all-reduce.5
